TPU v7x, 32 devices: a whole 2x2x4 slice. The times are simulated.
32 devices in a mesh: group: 2 (over x), tensor: 16 (over z, y, core).
Axes of the slice: x: 2, y: 2, z: 4, core: 2. Of those that a mesh axis runs over, the one named last changes fastest.
Arguments:
- hidden_in: bfloat16 [256, 2048], P(('group', 'tensor')), parts along dimension 0, may hold values from -6 to 6
- queries: bfloat16 [1024, 2048], P(('group', 'tensor')), parts along dimension 0, may hold values from -6 to 6
- kv_cache: bfloat16 [1024, 64, 256], P(('group', 'tensor')), parts along dimension 0, may hold values from -6 to 6
- new_kv: bfloat16 [1024, 256], P(('group', 'tensor')), parts along dimension 0, may hold values from -8 to 8
- cycle_pos: int32 [256], P('group'), parts along dimension 0, may hold values from 0 to 59
- out_weight: bfloat16 [8192, 2048], P('tensor'), may hold values from -0.125 to 0.125
- norm_gain: float32 [2048], replicated, may hold values from 0.1 to 1.9
- route_logits: float32 [256, 8], P(('group', 'tensor')), parts along dimension 0, may hold values from -6 to 303
- expert_ids: int32 [256, 8], P(('group', 'tensor')), parts along dimension 0, may hold values from 0 to 15, all different within a row; in each aligned block of 8 rows (0 to 7, 8 to 15, ...) at most 8 rows name the same one
- expert_in: bfloat16 [16, 2048, 1536], P('tensor'), may hold values from -0.125 to 0.125
- expert_out: bfloat16 [16, 768, 2048], P('tensor'), may hold values from -0.21875 to 0.21875
Outputs:
- hidden_out: bfloat16 [256, 2048], P(('group', 'tensor')), parts along dimension 0
- new_cache: bfloat16 [1024, 64, 256], P(('group', 'tensor')), parts along dimension 0
There are 2 independent parts, one for each index of `group`. A program takes and returns all parts, laid end to end along the dimension named above; an argument that names none is the same for every part. Nothing has to cross between parts.
Inputs may be any that keep to these rules, and one draw needn't show every extreme that they name: `expert_ids`: among the rows of one device no expert is named more than 8 times, a bound that some block reaches there in some device's rows. The 8 experts of a row differ.
All inputs are finite; a program needn't handle non-finite values.
Results may differ from a plain program's by a relative error of at most 0.0063.
Values may be sent and summed in bfloat16 or wider, within the bound.
A program may use at most 64 MiB of HBM per device.

v0:
```python
import math

import jax
import jax.numpy as jnp
from jax import lax
from jax.sharding import PartitionSpec as P

D = 2048
FF = 768
HD = 128
KVH = 4
HQ = 64
TOP = 8
SINK = 4
G = 16
SLOTS = 64


def expert_ffn(rows_in, expert_in, expert_out):
    joined = jnp.dot(rows_in, expert_in[0], preferred_element_type=jnp.float32)
    activated = (jax.nn.silu(joined[:, :FF]) * joined[:, FF:]).astype(jnp.bfloat16)
    return jnp.dot(activated, expert_out[0], preferred_element_type=jnp.float32).astype(
        jnp.bfloat16
    )


def on_device(
    hidden_in,
    queries,
    kv_cache,
    new_kv,
    cycle_pos,
    out_weight,
    norm_gain,
    route_logits,
    expert_ids,
    expert_in,
    expert_out,
):
    devices = lax.axis_size("tensor")
    device_index = lax.axis_index("tensor")
    rows_here = kv_cache.shape[0]
    local_tokens = hidden_in.shape[0]
    head_dev = HQ // devices
    own_pos = lax.dynamic_slice_in_dim(cycle_pos, device_index * local_tokens, local_tokens)
    positions = jnp.repeat(own_pos, KVH) + SINK
    write_mask = lax.broadcasted_iota(jnp.int32, (rows_here, SLOTS), 1) == positions[:, None]
    new_cache = jnp.where(write_mask[:, :, None], new_kv[:, None, :], kv_cache)
    key_part = new_cache[:, :, :HD]
    value_part = new_cache[:, :, HD:]
    query_heads = queries.reshape(rows_here, G, HD)
    scores = jnp.einsum(
        "rqk,rsk->rqs", query_heads, key_part, preferred_element_type=jnp.float32
    ) / math.sqrt(HD)
    peak = jnp.max(scores, axis=-1, keepdims=True)
    weights = jnp.exp(scores - peak)
    attn_probs = (weights / jnp.sum(weights, axis=-1, keepdims=True)).astype(jnp.bfloat16)
    head_out = jnp.einsum(
        "rqs,rsk->rqk", attn_probs, value_part, preferred_element_type=jnp.float32
    ).astype(jnp.bfloat16)
    by_head = head_out.reshape(local_tokens, devices, head_dev * HD)
    arrived = lax.all_to_all(by_head, "tensor", split_axis=1, concat_axis=0, tiled=True)
    own_heads = arrived.reshape(local_tokens * devices, head_dev * HD)
    attn_rows = lax.psum_scatter(
        jnp.dot(own_heads, out_weight, preferred_element_type=jnp.float32),
        "tensor",
        scatter_dimension=0,
        tiled=True,
    )
    mid_state = (hidden_in.astype(jnp.float32) + attn_rows).astype(jnp.bfloat16)
    mid_wide = mid_state.astype(jnp.float32)
    normed = (
        mid_wide
        * lax.rsqrt(jnp.mean(mid_wide * mid_wide, axis=-1, keepdims=True) + 1e-06)
        * norm_gain
    ).astype(jnp.bfloat16)
    gate_probs = jax.nn.softmax(route_logits, axis=-1).astype(jnp.bfloat16)
    capacity = min(local_tokens, max(2, 5 * local_tokens * TOP // devices))
    entries = expert_ids.reshape(-1)
    expert_table = (entries[:, None] == lax.broadcasted_iota(jnp.int32, (1, devices), 1)).astype(
        jnp.int32
    )
    before = jnp.cumsum(expert_table, axis=0) - expert_table
    slot_rank = jnp.sum(before * expert_table, axis=1)
    slot_flat = entries * capacity + slot_rank
    slot_table = (
        slot_flat[:, None] == lax.broadcasted_iota(jnp.int32, (1, devices * capacity), 1)
    ).reshape(local_tokens, TOP, devices * capacity)
    dispatch = jnp.any(slot_table, axis=1).astype(jnp.bfloat16)
    weighted = jnp.sum(
        jnp.where(slot_table, gate_probs.astype(jnp.float32)[:, :, None], 0.0), axis=1
    ).astype(jnp.bfloat16)
    outgoing = jnp.einsum("ic,id->cd", dispatch, normed, preferred_element_type=jnp.float32).astype(
        jnp.bfloat16
    )
    outgoing = outgoing.reshape(devices, capacity, D)
    incoming = lax.all_to_all(outgoing, "tensor", split_axis=0, concat_axis=0, tiled=True)
    result = expert_ffn(incoming.reshape(-1, D), expert_in, expert_out).reshape(incoming.shape)
    returned = lax.all_to_all(result, "tensor", split_axis=0, concat_axis=0, tiled=True)
    moe_total = jnp.dot(
        weighted, returned.reshape(devices * capacity, D), preferred_element_type=jnp.float32
    )
    hidden_out = (mid_state.astype(jnp.float32) + moe_total).astype(jnp.bfloat16)
    return (hidden_out, new_cache)


def solution(mesh):
    return jax.shard_map(
        on_device,
        mesh=mesh,
        in_specs=(
            P(("group", "tensor"), None),
            P(("group", "tensor"), None),
            P(("group", "tensor"), None, None),
            P(("group", "tensor"), None),
            P("group"),
            P("tensor", None),
            P(),
            P(("group", "tensor"), None),
            P(("group", "tensor"), None),
            P("tensor", None, None),
            P("tensor", None, None),
        ),
        out_specs=(P(("group", "tensor"), None), P(("group", "tensor"), None, None)),
        check_vma=False,
    )
```

profile of v0, /device:TPU:0, one launch (start us, length us, event | category | flops | bytes accessed | tf_op | source)
XLA Modules:
  0.0 140.0 jit_solution(6345263758116429869)
XLA Ops:
  7.2 0.0 copy-start
  7.2 0.0 reduce-scatter.2.cloned.1.call-start
  7.2 0.9 dynamic-slice_add_fusion
  8.1 0.1 broadcast_in_dim.26
  8.2 0.1 add.47
  8.3 0.1 iota_compare_fusion.2
  8.3 0.9 copy.15
  9.3 1.5 %broadcast_select_fusion = bf16[32,64,256]{2,1,0:T(8,128)(2,1)S(1)} fusion(bf16[32,64,256]{2,1,0:T(8,128)(2,1)} %param.13, pred[32,64]{1,0:T(8,128)(4,1)S(1)} %iota_compare_fusion.2, bf16[32,256]{1,0:T(8,128)(2,1)} %param.14), kind=kLoop, calls=%fused_computation.16 | loop fusion | flops 524288 | bytes 2115584 | tf_op jit(solution)/shard_map/jit(_where)/select_n | solution.py:48
  10.8 0.0 copy-start.1
  10.8 1.0 copy-done.1
  11.8 0.4 fusion.14
  12.1 0.2 fusion.39
  12.4 2.0 %convolution_convert_fusion.1 = bf16[32,16,128]{2,1,0:T(8,128)(2,1)S(1)} fusion(bf16[32,64,256]{2,1,0:T(8,128)(2,1)} %copy-done.1, f32[32,16]{1,0:T(8,128)S(1)} %fusion.39, f32[32,16,64]{2,1,0:T(8,128)S(1)} %fusion.14), kind=kOutput, calls=%fused_computation.15 | convolution fusion | flops 8553023 | bytes 1196032 | tf_op jit(solution)/shard_map/rqs,rsk->rqk/dot_general | solution.py:58
  14.4 0.0 copy-start.4
  14.4 0.0 copy-start.3
  14.4 0.0 copy-start.5
  14.4 0.1 reshape.87
  14.5 0.1 copy.14
  14.6 15.1 %all_to_all.25 = bf16[8,16,512]{2,0,1:T(8,128)(2,1)S(1)} all-to-all(bf16[8,16,512]{2,0,1:T(8,128)(2,1)S(1)} %copy.14), channel_id=1, replica_groups=mesh['group'=2,'tensor'=16] {'tensor'}, dimensions={1} | all-to-all | bytes 262144 | tf_op jit(solution)/shard_map/all_to_all | solution.py:62
  29.7 3.0 %fusion.23 = f32[128,2048]{1,0:T(8,128)} fusion(bf16[512,2048]{1,0:T(8,128)(2,1)} %param.16, bf16[8,16,512]{2,0,1:T(8,128)(2,1)S(1)} %all_to_all.25), kind=kOutput, calls=%fused_computation.25 | convolution fusion | flops 268435456 | bytes 3276800 | tf_op jit(solution)/shard_map/dot_general | solution.py:65
  32.7 0.0 reduce-scatter.2.cloned.1.call-update
  32.8 0.0 copy-done.4
  32.8 0.1 eq.43
  32.9 0.1 fusion.33
  32.9 0.1 reduce_window_sum.11
  33.0 0.2 select_reduce_fusion.1
  33.2 0.1 reduce_sum.49
  33.3 0.1 fusion.32
  33.4 54.9 %reduce-scatter.2.cloned.1.call-done = f32[8,2048]{1,0:T(8,128)} async-done(((f32[128,2048]{1,0:T(8,128)}), f32[8,2048]{1,0:T(8,128)}) %reduce-scatter.2.cloned.1.call-update) | async-done | bytes 65552 | tf_op jit(solution)/shard_map/reduce_scatter | solution.py:64
  88.3 0.0 copy-done.3
  88.3 1.0 fusion.26
  89.3 0.0 copy-done.5
  89.3 0.4 fusion.8
  89.6 17.9 %all_to_all.26 = bf16[16,8,2048]{2,1,0:T(8,128)(2,1)S(1)} all-to-all(bf16[16,8,2048]{2,1,0:T(8,128)(2,1)S(1)} %fusion.8), channel_id=1, replica_groups=mesh['group'=2,'tensor'=16] {'tensor'}, dimensions={0} | all-to-all | bytes 1048576 | tf_op jit(solution)/shard_map/all_to_all | solution.py:97
  107.5 3.8 %fusion.1 = f32[128,1536]{1,0:T(8,128)S(1)} fusion(bf16[1,2048,1536]{2,1,0:T(8,128)(2,1)} %param.20, bf16[16,8,2048]{2,1,0:T(8,128)(2,1)S(1)} %all_to_all.26), kind=kOutput, calls=%fused_computation.1 | convolution fusion | flops 805306368 | bytes 7602176 | tf_op jit(solution)/shard_map/dot_general | solution.py:20
  111.3 0.0 copy-done
  111.3 0.0 copy-start.2
  111.3 1.4 %fusion.9 = bf16[16,8,2048]{2,1,0:T(8,128)(2,1)} fusion(bf16[1,768,2048]{2,1,0:T(8,128)(2,1)S(1)} %copy-done, f32[128,1536]{1,0:T(8,128)S(1)} %fusion.1), kind=kOutput, calls=%fused_computation.8 | convolution fusion | flops 403505152 | bytes 4456448 | tf_op jit(solution)/shard_map/dot_general | solution.py:22
  112.7 4.2 %all-to-all-start.2 = ((bf16[16,8,2048]{2,1,0:T(8,128)(2,1)}), bf16[16,8,2048]{2,1,0:T(8,128)(2,1)}, u32[]{:S(2)}, u32[]{:S(2)}) async-start(bf16[16,8,2048]{2,1,0:T(8,128)(2,1)} %fusion.9), calls=%async_computation.3 | async-start | bytes 1048576 | tf_op jit(solution)/shard_map/all_to_all | solution.py:99
  117.0 0.0 copy-done.2
  117.0 0.1 reduce_max.19
  117.1 0.2 fusion.34
  117.3 0.1 fusion.35
  117.4 0.1 select_reduce_fusion
  117.5 13.8 %all-to-all-done.2 = bf16[16,8,2048]{2,1,0:T(8,128)(2,1)} async-done(((bf16[16,8,2048]{2,1,0:T(8,128)(2,1)}), bf16[16,8,2048]{2,1,0:T(8,128)(2,1)}, u32[]{:S(2)}, u32[]{:S(2)}) %all-to-all-start.2) | async-done | bytes 524320 | tf_op jit(solution)/shard_map/all_to_all | solution.py:99
  131.3 1.8 %fusion.12 = bf16[8,2048]{1,0:T(8,128)(2,1)} fusion(bf16[16,8,2048]{2,1,0:T(8,128)(2,1)} %all-to-all-done.2, bf16[8,2048]{1,0:T(8,128)(2,1)S(1)} %get-tuple-element.3, bf16[8,128]{1,0:T(8,128)(2,1)S(1)} %select_reduce_fusion), kind=kOutput, calls=%fused_computation.10 | convolution fusion | flops 4243456 | bytes 591872 | tf_op jit(solution)/shard_map/dot_general | solution.py:100
  (2 shorter events, 0.0 us)
Async XLA Ops:
  7.2 104.1 %copy-start = (bf16[1,768,2048]{2,1,0:T(8,128)(2,1)S(1)}, bf16[1,768,2048]{2,1,0:T(8,128)(2,1)}, u32[]{:S(2)}) copy-start(bf16[1,768,2048]{2,1,0:T(8,128)(2,1)} %param.21) | copy-start | bytes 9437188
  7.2 81.1 %reduce-scatter.2.cloned.1.call-start = ((), (), s32[]{:S(2)}) async-start(), calls=%async_computation.4 | async-start | bytes 1114112 | tf_op jit(solution)/shard_map/reduce_scatter | solution.py:64
  10.8 1.0 copy-start.1
  14.4 18.4 %copy-start.4 = (s32[8,8]{1,0:T(8,128)S(1)}, s32[8,8]{1,0:T(8,128)}, u32[]{:S(2)}) copy-start(s32[8,8]{1,0:T(8,128)} %param.19) | copy-start | bytes 772
  14.4 73.9 %copy-start.3 = (bf16[8,2048]{1,0:T(8,128)(2,1)S(1)}, bf16[8,2048]{1,0:T(8,128)(2,1)}, u32[]{:S(2)}) copy-start(bf16[8,2048]{1,0:T(8,128)(2,1)} %param.11) | copy-start | bytes 98308
  14.4 74.9 %copy-start.5 = (f32[2048]{0:T(1024)S(1)}, f32[2048]{0:T(1024)}, u32[]{:S(2)}) copy-start(f32[2048]{0:T(1024)} %param.17) | copy-start | bytes 24580
  111.3 5.7 %copy-start.2 = (f32[8,8]{1,0:T(8,128)S(1)}, f32[8,8]{1,0:T(8,128)}, u32[]{:S(2)}) copy-start(f32[8,8]{1,0:T(8,128)} %param.18) | copy-start | bytes 772
  112.7 18.5 %all-to-all-start.2 = ((bf16[16,8,2048]{2,1,0:T(8,128)(2,1)}), bf16[16,8,2048]{2,1,0:T(8,128)(2,1)}, u32[]{:S(2)}, u32[]{:S(2)}) async-start(bf16[16,8,2048]{2,1,0:T(8,128)(2,1)} %fusion.9), calls=%async_computation.3 | async-start | bytes 1048576 | tf_op jit(solution)/shard_map/all_to_all | solution.py:99
Sparse Core Ops, SparseCore 0:
  32.9 55.3 reduce-scatter.1
where the time goes:
time: 141 us; the launch traced here: 140 us
  waiting for transfers between devices  68.7 us (49%)
  blocking collectives  33 us (23%)
  between operations  14.2 us (10%)
  matrix products  12.8 us (9%)
  other arithmetic  4.64 us (3%)
  starting transfers between devices  4.28 us (3%)
  local copies, waits for them, and re-layouts  2.41 us (2%)
    reduce_scatter x1, waiting for transfers between devices, on_device(): lax.psum_scatter(jnp.dot(own_heads, out_weight, preferred_element_type=jn...  54.9 us
    all_to_all x1, blocking collectives, on_device(): lax.all_to_all(outgoing, 'tensor', split_axis=0, concat_axis=0, tiled=True)  17.9 us
    all_to_all x1, blocking collectives, on_device(): lax.all_to_all(by_head, 'tensor', split_axis=1, concat_axis=0, tiled=True)  15.1 us
    all_to_all x1, waiting for transfers between devices, on_device(): lax.all_to_all(result, 'tensor', split_axis=0, concat_axis=0, tiled=True)  13.8 us
    all_to_all x1, starting transfers between devices, on_device(): lax.all_to_all(result, 'tensor', split_axis=0, concat_axis=0, tiled=True)  4.24 us
    dot_general x1, matrix products, expert_ffn(): joined = jnp.dot(rows_in, expert_in[0], preferred_element_type=jnp.float32)  3.78 us
    dot_general x1, matrix products, on_device(): jnp.dot(own_heads, out_weight, preferred_element_type=jnp.float32)  3.03 us
  transfers between devices with their start and end apart: 2, of which 2 were waited for; matrix products, arithmetic and copies ran while one was open for 1% of the time, Pallas kernels for 0%

commit v1 on v0

v1 whole, which is shorter than its diff:
```python
import functools
import math

import jax
import jax.numpy as jnp
from jax import lax
from jax.experimental import pallas as pl
from jax.experimental.pallas import tpu as pltpu
from jax.sharding import PartitionSpec as P

HD = 128
SINK = 4
CHUNKS = 4
MESH = pl.DeviceIdType.MESH


def wait_bytes(ref, sem):
    pltpu.make_async_copy(ref, ref, sem).wait()


def layer_kernel(
    n,
    by_head,
    hidden_in,
    norm_gain,
    route_logits,
    expert_ids,
    out_weight,
    expert_in,
    expert_out,
    hidden_out,
    w_proj,
    w_in,
    w_out,
    heads,
    core_out,
    core_in,
    mine,
    chip_out,
    chip_in,
    gathered,
    act,
    load_sem,
    head_send,
    head_recv,
    core_send,
    core_recv,
    chip_send,
    chip_recv,
    ag_send,
    ag_recv,
    relay_send,
    relay_recv,
):
    me = lax.axis_index("tensor")
    chips = n // 2
    chip, core = me // 2, me % 2
    partner = chip * 2 + (1 - core)
    tokens, width = hidden_in.shape
    part = width // CHUNKS
    ff = w_out.shape[0]
    half = chips * tokens

    barrier = pltpu.get_barrier_semaphore()

    @pl.loop(1, n)
    def _(k):
        pl.semaphore_signal(
            barrier, inc=1, device_id={"tensor": lax.rem(me + k, n)}, device_id_type=MESH
        )

    loads = [
        pltpu.make_async_copy(out_weight, w_proj, load_sem.at[0]),
        pltpu.make_async_copy(expert_in.at[0], w_in, load_sem.at[1]),
        pltpu.make_async_copy(expert_out.at[0], w_out, load_sem.at[2]),
    ]
    for load in loads:
        load.start()
    pl.semaphore_wait(barrier, n - 1)

    def slot(device):
        return lax.rem(device, 2) * chips + device // 2

    my_slot = slot(me)

    @pl.loop(1, n)
    def _(k):
        to = lax.rem(me + k, n)
        pltpu.make_async_remote_copy(
            src_ref=by_head.at[to],
            dst_ref=heads.at[my_slot],
            send_sem=head_send,
            recv_sem=head_recv,
            device_id={"tensor": to},
            device_id_type=MESH,
        ).start()

    heads[my_slot] = by_head[me]

    logits = route_logits[...]
    top = logits.shape[1]
    powers = jnp.exp(logits - jnp.max(logits, axis=-1, keepdims=True))
    gate = (powers / jnp.sum(powers, axis=-1, keepdims=True)).astype(jnp.bfloat16)
    gate = gate.astype(jnp.float32)
    pad = gathered.shape[2] - width
    lanes = lax.broadcasted_iota(jnp.int32, (tokens, pad), 1)
    ids = expert_ids[...]
    table = jnp.zeros((tokens, pad), jnp.float32)
    for j in range(top):
        table = table + jnp.where(lanes == ids[:, j : j + 1], gate[:, j : j + 1], 0.0)
    gathered[my_slot, :, width:] = table.astype(jnp.bfloat16)

    def rows_of(ref, lo, hi):
        other = ref[pl.ds((1 - core) * chips, chips), :, lo:hi].astype(jnp.float32)
        own = ref[pl.ds(core * chips, chips), :, lo:hi].astype(jnp.float32)
        return jnp.concatenate(
            [other.reshape(half, hi - lo), own.reshape(half, hi - lo)], axis=0
        )

    def core_copy(r, k):
        return pltpu.make_async_remote_copy(
            src_ref=core_out.at[r, k],
            dst_ref=core_in.at[r, k],
            send_sem=core_send.at[r, k],
            recv_sem=core_recv.at[r, k],
            device_id={"tensor": partner},
            device_id_type=MESH,
        )

    def reduce_scatter(r, term):
        for k in range(CHUNKS):
            value = term(k)
            core_out[r, k] = value[:half].reshape(chips, tokens, part).astype(jnp.bfloat16)
            core_copy(r, k).start()
            mine[k] = value[half:].reshape(chips, tokens, part)
        for k in range(CHUNKS):
            core_copy(r, k).wait_recv()
            both = (mine[k] + core_in[r, k].astype(jnp.float32)).astype(jnp.bfloat16)
            chip_out[r, k] = both

            @pl.loop(1, chips)
            def _(step):
                to = lax.rem(chip + step, chips)
                pltpu.make_async_remote_copy(
                    src_ref=chip_out.at[r, k, to],
                    dst_ref=chip_in.at[r, k, chip],
                    send_sem=chip_send.at[r],
                    recv_sem=chip_recv.at[r, k],
                    device_id={"tensor": to * 2 + core},
                    device_id_type=MESH,
                ).start()

            chip_in[r, k, chip] = chip_out[r, k, chip]
        sums = []
        for k in range(CHUNKS):
            wait_bytes(chip_in.at[r, k, pl.ds(0, chips - 1)], chip_recv.at[r, k])
            sums.append(jnp.sum(chip_in[r, k].astype(jnp.float32), axis=0))
        return jnp.concatenate(sums, axis=-1)

    wait_bytes(heads.at[pl.ds(0, n - 1)], head_recv)
    loads[0].wait()
    own_heads = rows_of(heads, 0, heads.shape[2]).astype(jnp.bfloat16)
    attn_rows = reduce_scatter(
        0,
        lambda k: jnp.dot(
            own_heads, w_proj[:, k * part : (k + 1) * part], preferred_element_type=jnp.float32
        ),
    )

    mid_state = (hidden_in[...].astype(jnp.float32) + attn_rows).astype(jnp.bfloat16)
    mid_wide = mid_state.astype(jnp.float32)
    scale = lax.rsqrt(jnp.mean(mid_wide * mid_wide, axis=-1, keepdims=True) + 1e-06)
    gathered[my_slot, :, :width] = (mid_wide * scale * norm_gain[...]).astype(jnp.bfloat16)

    @pl.loop(1, chips)
    def _(step):
        to = lax.rem(chip + step, chips)
        pltpu.make_async_remote_copy(
            src_ref=gathered.at[my_slot],
            dst_ref=gathered.at[my_slot],
            send_sem=ag_send,
            recv_sem=ag_recv.at[chip],
            device_id={"tensor": to * 2 + core},
            device_id_type=MESH,
        ).start()

    def relay(index):
        pltpu.make_async_remote_copy(
            src_ref=gathered.at[index],
            dst_ref=gathered.at[index],
            send_sem=relay_send,
            recv_sem=relay_recv,
            device_id={"tensor": partner},
            device_id_type=MESH,
        ).start()

    relay(my_slot)

    @pl.loop(1, chips)
    def _(step):
        source = lax.rem(chip + step, chips)
        index = core * chips + source
        wait_bytes(gathered.at[index], ag_recv.at[source])
        relay(index)

    wait_bytes(gathered.at[pl.ds(0, chips)], relay_recv)

    lane = lax.broadcasted_iota(jnp.int32, (2 * half, pad), 1)
    share = jnp.sum(
        jnp.where(lane == me, rows_of(gathered, width, width + pad), 0.0), axis=-1, keepdims=True
    )
    rows_in = rows_of(gathered, 0, width).astype(jnp.bfloat16)
    loads[1].wait()
    piece = 256
    for lo in range(0, ff, piece):
        gate_part = jnp.dot(
            rows_in, w_in[:, lo : lo + piece], preferred_element_type=jnp.float32
        )
        up_part = jnp.dot(
            rows_in, w_in[:, ff + lo : ff + lo + piece], preferred_element_type=jnp.float32
        )
        act[:, lo : lo + piece] = (gate_part / (1.0 + jnp.exp(-gate_part)) * up_part).astype(
            jnp.bfloat16
        )
    loads[2].wait()

    def expert_term(k):
        result = jnp.dot(
            act[...], w_out[:, k * part : (k + 1) * part], preferred_element_type=jnp.float32
        )
        return result.astype(jnp.bfloat16).astype(jnp.float32) * share

    moe_total = reduce_scatter(1, expert_term)
    hidden_out[...] = (mid_wide + moe_total).astype(jnp.bfloat16)

    wait_bytes(heads.at[pl.ds(0, n - 1)], head_send)
    for r in range(2):
        for k in range(CHUNKS):
            core_copy(r, k).wait_send()
        wait_bytes(chip_out.at[r, :, pl.ds(0, chips - 1)], chip_send.at[r])
    wait_bytes(gathered.at[pl.ds(0, chips - 1)], ag_send)
    wait_bytes(gathered.at[pl.ds(0, chips)], relay_send)


def layer(n, by_head, hidden_in, norm_gain, route_logits, expert_ids, weights):
    tokens, width = hidden_in.shape
    out_weight, expert_in, expert_out = weights
    ff = expert_out.shape[1]
    chips = n // 2
    pad = -(-n // 128) * 128
    part = width // CHUNKS
    bf16, f32 = jnp.bfloat16, jnp.float32
    vmem = pl.BlockSpec(memory_space=pltpu.VMEM)
    hbm = pl.BlockSpec(memory_space=pl.ANY)
    dma = pltpu.SemaphoreType.DMA
    return pl.pallas_call(
        functools.partial(layer_kernel, n),
        out_shape=jax.ShapeDtypeStruct((tokens, width), bf16),
        in_specs=[vmem] * 5 + [hbm] * 3,
        out_specs=vmem,
        scratch_shapes=[
            pltpu.VMEM(out_weight.shape, bf16),
            pltpu.VMEM(expert_in.shape[1:], bf16),
            pltpu.VMEM(expert_out.shape[1:], bf16),
            pltpu.VMEM(by_head.shape, bf16),
            pltpu.VMEM((2, CHUNKS, chips, tokens, part), bf16),
            pltpu.VMEM((2, CHUNKS, chips, tokens, part), bf16),
            pltpu.VMEM((CHUNKS, chips, tokens, part), f32),
            pltpu.VMEM((2, CHUNKS, chips, tokens, part), bf16),
            pltpu.VMEM((2, CHUNKS, chips, tokens, part), bf16),
            pltpu.VMEM((n, tokens, width + pad), bf16),
            pltpu.VMEM((n * tokens, ff), bf16),
            dma((3,)),
            dma,
            dma,
            dma((2, CHUNKS)),
            dma((2, CHUNKS)),
            dma((2,)),
            dma((2, CHUNKS)),
            dma,
            dma((chips,)),
            dma,
            dma,
        ],
        compiler_params=pltpu.CompilerParams(
            collective_id=0, has_side_effects=True, vmem_limit_bytes=60 * 1024 * 1024
        ),
        name="layer",
    )(by_head, hidden_in, norm_gain, route_logits, expert_ids, out_weight, expert_in, expert_out)


def on_device(
    hidden_in,
    queries,
    kv_cache,
    new_kv,
    cycle_pos,
    out_weight,
    norm_gain,
    route_logits,
    expert_ids,
    expert_in,
    expert_out,
):
    devices = lax.axis_size("tensor")
    device_index = lax.axis_index("tensor")
    rows_here, slots, _ = kv_cache.shape
    local_tokens = hidden_in.shape[0]
    kv_heads = rows_here // local_tokens
    per_kv = queries.shape[1] // HD
    head_dev = kv_heads * per_kv // devices
    own_pos = lax.dynamic_slice_in_dim(cycle_pos, device_index * local_tokens, local_tokens)
    positions = jnp.repeat(own_pos, kv_heads) + SINK
    write_mask = lax.broadcasted_iota(jnp.int32, (rows_here, slots), 1) == positions[:, None]
    new_cache = jnp.where(write_mask[:, :, None], new_kv[:, None, :], kv_cache)
    key_part = new_cache[:, :, :HD]
    value_part = new_cache[:, :, HD:]
    query_heads = queries.reshape(rows_here, per_kv, HD)
    scores = jnp.einsum(
        "rqk,rsk->rqs", query_heads, key_part, preferred_element_type=jnp.float32
    ) / math.sqrt(HD)
    peak = jnp.max(scores, axis=-1, keepdims=True)
    weights = jnp.exp(scores - peak)
    attn_probs = (weights / jnp.sum(weights, axis=-1, keepdims=True)).astype(jnp.bfloat16)
    head_out = jnp.einsum(
        "rqs,rsk->rqk", attn_probs, value_part, preferred_element_type=jnp.float32
    ).astype(jnp.bfloat16)
    by_head = head_out.reshape(local_tokens, devices, head_dev * HD).transpose(1, 0, 2)
    hidden_out = layer(
        devices,
        by_head,
        hidden_in,
        norm_gain.reshape(1, -1),
        route_logits,
        expert_ids,
        (out_weight, expert_in, expert_out),
    )
    return (hidden_out, new_cache)


def solution(mesh):
    return jax.shard_map(
        on_device,
        mesh=mesh,
        in_specs=(
            P(("group", "tensor"), None),
            P(("group", "tensor"), None),
            P(("group", "tensor"), None, None),
            P(("group", "tensor"), None),
            P("group"),
            P("tensor", None),
            P(),
            P(("group", "tensor"), None),
            P(("group", "tensor"), None),
            P("tensor", None, None),
            P("tensor", None, None),
        ),
        out_specs=(P(("group", "tensor"), None), P(("group", "tensor"), None, None)),
        check_vma=False,
    )
```

time: 141 us -> 49 us (0.35)
  waiting for transfers between devices: 68.7 us -> 0 us
  Pallas kernels: 0 us -> 40.9 us
  blocking collectives: 33 us -> 0 us
  between operations: 14.2 us -> 0.69 us
  matrix products: 12.8 us -> 1.34 us
  starting transfers between devices: 4.28 us -> 0 us
  other arithmetic: 4.64 us -> 2.55 us
    reduce_scatter x1 -> x0, waiting for transfers between devices: 54.9 us -> none  [on_device(): lax.psum_scatter(jnp.dot(own_heads, out_weight, preferred_element_type=jn...]
    pallas_call x0 -> x1, Pallas kernels: none -> 40.9 us  [layer(): pl.pallas_call(functools.partial(layer_kernel, n), out_shape=jax.ShapeDty...]
    all_to_all x2 -> x0, blocking collectives: 33 us -> none  [the longest x1 17.9 us: on_device(): lax.all_to_all(outgoing, 'tensor', split_axis=0, concat_axis=0, tiled=True)]
    all_to_all x1 -> x0, waiting for transfers between devices: 13.8 us -> none  [on_device(): lax.all_to_all(result, 'tensor', split_axis=0, concat_axis=0, tiled=True)]
    dot_general x5 -> x0, matrix products: 10.4 us -> none  [the longest x1 3.78 us: expert_ffn(): joined = jnp.dot(rows_in, expert_in[0], preferred_element_type=jnp.float32)]
    all_to_all x1 -> x0, starting transfers between devices: 4.24 us -> none  [on_device(): lax.all_to_all(result, 'tensor', split_axis=0, concat_axis=0, tiled=True)]
    reduce_sum x4 -> x0, other arithmetic: 1.44 us -> none  [the longest x1 0.97 us: on_device(): jnp.mean(mid_wide * mid_wide, axis=-1, keepdims=True) + 1e-06]
  transfers between devices with their start and end apart: 2 -> 0, of which waited for: 2 -> 0; matrix products, arithmetic and copies ran while one was open for 1% -> 0% of each run, Pallas kernels for 0% -> 0%
where the time goes in v1:
time: 49 us; the launch traced here: 48.7 us
  Pallas kernels  40.9 us (83%)
  local copies, waits for them, and re-layouts  3.28 us (7%)
  other arithmetic  2.55 us (5%)
  matrix products  1.34 us (3%)
  between operations  0.69 us (1%)
    pallas_call x1, Pallas kernels, layer(): pl.pallas_call(functools.partial(layer_kernel, n), out_shape=jax.ShapeDty...  40.9 us
    unnamed x4, local copies, waits for them, and re-layouts  2.31 us
    select_n x1, other arithmetic, on_device(): new_cache = jnp.where(write_mask[:, :, None], new_kv[:, None, :], kv_cache)  1.51 us

profile of v1, /device:TPU:0, one launch (start us, length us, event | category | flops | bytes accessed | tf_op | source)
XLA Modules:
  0.0 48.7 jit_solution(8289463794967596298)
XLA Ops:
  0.6 0.7 %dynamic-slice_add_fusion = s32[8]{0:T(128)S(1)} fusion(s32[128]{0:T(128)} %param.15, s32[]{:T(128)S(6)} %select_n.7), kind=kLoop, calls=%fused_computation.14 | loop fusion | flops 8 | bytes 68 | tf_op jit(solution)/shard_map/add | solution.py:313
  1.4 0.1 broadcast_in_dim.24
  1.4 0.1 add.20
  1.5 0.1 iota_compare_fusion
  1.6 0.9 %copy.14 = bf16[4,8,16,128]{3,2,1,0:T(8,128)(2,1)S(1)} copy(bf16[4,8,16,128]{3,1,2,0:T(8,128)(2,1)} %bitcast.13) | data formatting | bytes 262144
  2.5 1.5 %broadcast_select_fusion = bf16[32,64,256]{2,1,0:T(8,128)(2,1)S(1)} fusion(bf16[32,64,256]{2,1,0:T(8,128)(2,1)} %param.13, pred[32,64]{1,0:T(8,128)(4,1)S(1)} %iota_compare_fusion, bf16[32,256]{1,0:T(8,128)(2,1)} %param.14), kind=kLoop, calls=%fused_computation.6 | loop fusion | flops 524288 | bytes 2115584 | tf_op jit(solution)/shard_map/jit(_where)/select_n | solution.py:315
  4.0 0.0 copy-start
  4.1 0.4 fusion.2
  4.4 0.2 fusion.8
  4.7 1.0 %convolution_convert_fusion = bf16[32,16,128]{2,1,0:T(8,128)(2,1)S(1)} fusion(bf16[32,64,256]{2,1,0:T(8,128)(2,1)S(1)} %broadcast_select_fusion, f32[32,16]{1,0:T(8,128)S(1)} %fusion.8, f32[32,16,64]{2,1,0:T(8,128)S(1)} %fusion.2), kind=kOutput, calls=%fused_computation.5 | convolution fusion | flops 8553023 | bytes 1196032 | tf_op jit(solution)/shard_map/rqs,rsk->rqk/dot_general | solution.py:325
  5.6 0.1 reshape.43
  5.7 0.7 %copy.16 = bf16[8,16,512]{2,0,1:T(8,128)(2,1)} copy(bf16[8,16,512]{2,1,0:T(8,128)(2,1)S(1)} %reshape.43) | data formatting | bytes 262144 | tf_op jit(solution)/shard_map/reshape | solution.py:328
  6.5 40.9 %layer.1 = bf16[8,2048]{1,0:T(8,128)(2,1)} custom-call(bf16[16,8,512]{2,1,0:T(8,128)(2,1)} %bitcast.11, bf16[8,2048]{1,0:T(8,128)(2,1)} %hidden_in.1, f32[1,2048]{1,0:T(1,128)} %bitcast.14, f32[8,8]{1,0:T(8,128)} %route_logits.1, s32[8,8]{1,0:T(8,128)} %expert_ids.1, bf16[512,2048]{1,0:T(8,128)(2,1)} %out_weight.1, bf16[1,2048,1536]{2,1,0:T(8,128)(2,1)} %expert_in.1, ...), custom_call_target="tpu_custom_call" | custom-call | tf_op jit(solution)/shard_map/layer/pallas_call | solution.py:256
  47.3 0.0 copy-done
  47.3 1.4 %copy.18 = bf16[8,2048]{1,0:T(8,128)(2,1)} copy(bf16[8,2048]{1,0:T(8,128)(2,1)} %layer.1) | data formatting | bytes 65536
Async XLA Ops:
  4.0 43.3 %copy-start = (bf16[32,64,256]{2,1,0:T(8,128)(2,1)}, bf16[32,64,256]{2,1,0:T(8,128)(2,1)S(1)}, u32[]{:S(2)}) copy-start(bf16[32,64,256]{2,1,0:T(8,128)(2,1)S(1)} %broadcast_select_fusion) | copy-start | bytes 3145732

commit v2 on v1

--- a/solution.py
+++ b/solution.py
@@ -10,7 +10,6 @@
 
 HD = 128
 SINK = 4
-CHUNKS = 4
 MESH = pl.DeviceIdType.MESH
 
 
@@ -20,11 +19,12 @@
 
 def layer_kernel(
     n,
-    by_head,
+    queries,
     hidden_in,
     norm_gain,
     route_logits,
     expert_ids,
+    new_cache,
     out_weight,
     expert_in,
     expert_out,
@@ -32,6 +32,11 @@
     w_proj,
     w_in,
     w_out,
+    cache,
+    query_rows,
+    score_rows,
+    out_rows,
+    by_head,
     heads,
     core_out,
     core_in,
@@ -57,7 +62,6 @@
     chip, core = me // 2, me % 2
     partner = chip * 2 + (1 - core)
     tokens, width = hidden_in.shape
-    part = width // CHUNKS
     ff = w_out.shape[0]
     half = chips * tokens
 
@@ -69,6 +73,8 @@
             barrier, inc=1, device_id={"tensor": lax.rem(me + k, n)}, device_id_type=MESH
         )
 
+    cache_load = pltpu.make_async_copy(new_cache, cache, load_sem.at[3])
+    cache_load.start()
     loads = [
         pltpu.make_async_copy(out_weight, w_proj, load_sem.at[0]),
         pltpu.make_async_copy(expert_in.at[0], w_in, load_sem.at[1]),
@@ -76,6 +82,34 @@
     ]
     for load in loads:
         load.start()
+
+    rows_here = cache.shape[0]
+    kv_heads = rows_here // tokens
+    per_kv = queries.shape[1] // HD
+    for h in range(per_kv):
+        query_rows[h * rows_here : (h + 1) * rows_here, :] = queries[
+            :, h * HD : (h + 1) * HD
+        ].astype(jnp.float32)
+    cache_load.wait()
+    for r in range(rows_here):
+        query = query_rows[pl.ds(r, per_kv, stride=rows_here), :].astype(jnp.bfloat16)
+        score_rows[r * per_kv : (r + 1) * per_kv, :] = lax.dot_general(
+            query,
+            cache[r, :, :HD],
+            (((1,), (1,)), ((), ())),
+            preferred_element_type=jnp.float32,
+        )
+    scores = score_rows[...] / math.sqrt(HD)
+    powers = jnp.exp(scores - jnp.max(scores, axis=-1, keepdims=True))
+    score_rows[...] = powers / jnp.sum(powers, axis=-1, keepdims=True)
+    for r in range(rows_here):
+        probs = score_rows[r * per_kv : (r + 1) * per_kv, :].astype(jnp.bfloat16)
+        first = (r % kv_heads) * per_kv * tokens + r // kv_heads
+        out_rows[pl.ds(first, per_kv, stride=tokens), :] = jnp.dot(
+            probs, cache[r, :, HD:], preferred_element_type=jnp.float32
+        )
+    by_head[...] = out_rows[...].reshape(by_head.shape).astype(jnp.bfloat16)
+
     pl.semaphore_wait(barrier, n - 1)
 
     def slot(device):
@@ -117,55 +151,55 @@
             [other.reshape(half, hi - lo), own.reshape(half, hi - lo)], axis=0
         )
 
-    def core_copy(r, k):
+    def head_rows(parity):
+        block = heads[pl.ds(parity * chips, chips)].astype(jnp.float32)
+        return jnp.concatenate(
+            [block[:, h].reshape(half, HD) for h in range(heads.shape[1])], axis=-1
+        ).astype(jnp.bfloat16)
+
+    def core_copy(r):
         return pltpu.make_async_remote_copy(
-            src_ref=core_out.at[r, k],
-            dst_ref=core_in.at[r, k],
-            send_sem=core_send.at[r, k],
-            recv_sem=core_recv.at[r, k],
+            src_ref=core_out.at[r],
+            dst_ref=core_in.at[r],
+            send_sem=core_send.at[r],
+            recv_sem=core_recv.at[r],
             device_id={"tensor": partner},
             device_id_type=MESH,
         )
 
-    def reduce_scatter(r, term):
-        for k in range(CHUNKS):
-            value = term(k)
-            core_out[r, k] = value[:half].reshape(chips, tokens, part).astype(jnp.bfloat16)
-            core_copy(r, k).start()
-            mine[k] = value[half:].reshape(chips, tokens, part)
-        for k in range(CHUNKS):
-            core_copy(r, k).wait_recv()
-            both = (mine[k] + core_in[r, k].astype(jnp.float32)).astype(jnp.bfloat16)
-            chip_out[r, k] = both
-
-            @pl.loop(1, chips)
-            def _(step):
-                to = lax.rem(chip + step, chips)
-                pltpu.make_async_remote_copy(
-                    src_ref=chip_out.at[r, k, to],
-                    dst_ref=chip_in.at[r, k, chip],
-                    send_sem=chip_send.at[r],
-                    recv_sem=chip_recv.at[r, k],
-                    device_id={"tensor": to * 2 + core},
-                    device_id_type=MESH,
-                ).start()
-
-            chip_in[r, k, chip] = chip_out[r, k, chip]
-        sums = []
-        for k in range(CHUNKS):
-            wait_bytes(chip_in.at[r, k, pl.ds(0, chips - 1)], chip_recv.at[r, k])
-            sums.append(jnp.sum(chip_in[r, k].astype(jnp.float32), axis=0))
-        return jnp.concatenate(sums, axis=-1)
+    def reduce_scatter(r, other_term, own_term):
+        core_out[r] = other_term().reshape(chips, tokens, width).astype(jnp.bfloat16)
+        core_copy(r).start()
+        mine[...] = own_term().reshape(chips, tokens, width)
+        core_copy(r).wait_recv()
+
+        def total(to):
+            return (mine[to] + core_in[r, to].astype(jnp.float32)).astype(jnp.bfloat16)
+
+        @pl.loop(1, chips)
+        def _(step):
+            to = lax.rem(chip + step, chips)
+            chip_out[r, to] = total(to)
+            pltpu.make_async_remote_copy(
+                src_ref=chip_out.at[r, to],
+                dst_ref=chip_in.at[r, chip],
+                send_sem=chip_send.at[r],
+                recv_sem=chip_recv.at[r],
+                device_id={"tensor": to * 2 + core},
+                device_id_type=MESH,
+            ).start()
+
+        chip_in[r, chip] = total(chip)
+        wait_bytes(chip_in.at[r, pl.ds(0, chips - 1)], chip_recv.at[r])
+        return jnp.sum(chip_in[r].astype(jnp.float32), axis=0)
 
     wait_bytes(heads.at[pl.ds(0, n - 1)], head_recv)
     loads[0].wait()
-    own_heads = rows_of(heads, 0, heads.shape[2]).astype(jnp.bfloat16)
-    attn_rows = reduce_scatter(
-        0,
-        lambda k: jnp.dot(
-            own_heads, w_proj[:, k * part : (k + 1) * part], preferred_element_type=jnp.float32
-        ),
-    )
+
+    def projected(parity):
+        return jnp.dot(head_rows(parity), w_proj[...], preferred_element_type=jnp.float32)
+
+    attn_rows = reduce_scatter(0, lambda: projected(1 - core), lambda: projected(core))
 
     mid_state = (hidden_in[...].astype(jnp.float32) + attn_rows).astype(jnp.bfloat16)
     mid_wide = mid_state.astype(jnp.float32)
@@ -224,31 +258,32 @@
         )
     loads[2].wait()
 
-    def expert_term(k):
+    def expert_term(lo):
         result = jnp.dot(
-            act[...], w_out[:, k * part : (k + 1) * part], preferred_element_type=jnp.float32
-        )
-        return result.astype(jnp.bfloat16).astype(jnp.float32) * share
-
-    moe_total = reduce_scatter(1, expert_term)
+            act[lo : lo + half, :], w_out[...], preferred_element_type=jnp.float32
+        )
+        return result.astype(jnp.bfloat16).astype(jnp.float32) * share[lo : lo + half]
+
+    moe_total = reduce_scatter(1, lambda: expert_term(0), lambda: expert_term(half))
     hidden_out[...] = (mid_wide + moe_total).astype(jnp.bfloat16)
 
     wait_bytes(heads.at[pl.ds(0, n - 1)], head_send)
     for r in range(2):
-        for k in range(CHUNKS):
-            core_copy(r, k).wait_send()
-        wait_bytes(chip_out.at[r, :, pl.ds(0, chips - 1)], chip_send.at[r])
+        core_copy(r).wait_send()
+        wait_bytes(chip_out.at[r, pl.ds(0, chips - 1)], chip_send.at[r])
     wait_bytes(gathered.at[pl.ds(0, chips - 1)], ag_send)
     wait_bytes(gathered.at[pl.ds(0, chips)], relay_send)
 
 
-def layer(n, by_head, hidden_in, norm_gain, route_logits, expert_ids, weights):
+def layer(n, queries, hidden_in, norm_gain, route_logits, expert_ids, new_cache, weights):
     tokens, width = hidden_in.shape
     out_weight, expert_in, expert_out = weights
     ff = expert_out.shape[1]
     chips = n // 2
     pad = -(-n // 128) * 128
-    part = width // CHUNKS
+    rows_here, slots, _ = new_cache.shape
+    heads_all = rows_here // tokens * (queries.shape[1] // HD)
+    exchange = (n, heads_all // n, tokens, HD)
     bf16, f32 = jnp.bfloat16, jnp.float32
     vmem = pl.BlockSpec(memory_space=pltpu.VMEM)
     hbm = pl.BlockSpec(memory_space=pl.ANY)
@@ -256,27 +291,32 @@
     return pl.pallas_call(
         functools.partial(layer_kernel, n),
         out_shape=jax.ShapeDtypeStruct((tokens, width), bf16),
-        in_specs=[vmem] * 5 + [hbm] * 3,
+        in_specs=[vmem] * 5 + [hbm] * 4,
         out_specs=vmem,
         scratch_shapes=[
             pltpu.VMEM(out_weight.shape, bf16),
             pltpu.VMEM(expert_in.shape[1:], bf16),
             pltpu.VMEM(expert_out.shape[1:], bf16),
-            pltpu.VMEM(by_head.shape, bf16),
-            pltpu.VMEM((2, CHUNKS, chips, tokens, part), bf16),
-            pltpu.VMEM((2, CHUNKS, chips, tokens, part), bf16),
-            pltpu.VMEM((CHUNKS, chips, tokens, part), f32),
-            pltpu.VMEM((2, CHUNKS, chips, tokens, part), bf16),
-            pltpu.VMEM((2, CHUNKS, chips, tokens, part), bf16),
+            pltpu.VMEM(new_cache.shape, bf16),
+            pltpu.VMEM((heads_all * tokens, HD), f32),
+            pltpu.VMEM((heads_all * tokens, slots), f32),
+            pltpu.VMEM((heads_all * tokens, HD), f32),
+            pltpu.VMEM(exchange, bf16),
+            pltpu.VMEM(exchange, bf16),
+            pltpu.VMEM((2, chips, tokens, width), bf16),
+            pltpu.VMEM((2, chips, tokens, width), bf16),
+            pltpu.VMEM((chips, tokens, width), f32),
+            pltpu.VMEM((2, chips, tokens, width), bf16),
+            pltpu.VMEM((2, chips, tokens, width), bf16),
             pltpu.VMEM((n, tokens, width + pad), bf16),
             pltpu.VMEM((n * tokens, ff), bf16),
-            dma((3,)),
+            dma((4,)),
             dma,
             dma,
-            dma((2, CHUNKS)),
-            dma((2, CHUNKS)),
             dma((2,)),
-            dma((2, CHUNKS)),
+            dma((2,)),
+            dma((2,)),
+            dma((2,)),
             dma,
             dma((chips,)),
             dma,
@@ -286,7 +326,17 @@
             collective_id=0, has_side_effects=True, vmem_limit_bytes=60 * 1024 * 1024
         ),
         name="layer",
-    )(by_head, hidden_in, norm_gain, route_logits, expert_ids, out_weight, expert_in, expert_out)
+    )(
+        queries,
+        hidden_in,
+        norm_gain,
+        route_logits,
+        expert_ids,
+        new_cache,
+        out_weight,
+        expert_in,
+        expert_out,
+    )
 
 
 def on_device(
@@ -307,32 +357,22 @@
     rows_here, slots, _ = kv_cache.shape
     local_tokens = hidden_in.shape[0]
     kv_heads = rows_here // local_tokens
-    per_kv = queries.shape[1] // HD
-    head_dev = kv_heads * per_kv // devices
     own_pos = lax.dynamic_slice_in_dim(cycle_pos, device_index * local_tokens, local_tokens)
-    positions = jnp.repeat(own_pos, kv_heads) + SINK
-    write_mask = lax.broadcasted_iota(jnp.int32, (rows_here, slots), 1) == positions[:, None]
-    new_cache = jnp.where(write_mask[:, :, None], new_kv[:, None, :], kv_cache)
-    key_part = new_cache[:, :, :HD]
-    value_part = new_cache[:, :, HD:]
-    query_heads = queries.reshape(rows_here, per_kv, HD)
-    scores = jnp.einsum(
-        "rqk,rsk->rqs", query_heads, key_part, preferred_element_type=jnp.float32
-    ) / math.sqrt(HD)
-    peak = jnp.max(scores, axis=-1, keepdims=True)
-    weights = jnp.exp(scores - peak)
-    attn_probs = (weights / jnp.sum(weights, axis=-1, keepdims=True)).astype(jnp.bfloat16)
-    head_out = jnp.einsum(
-        "rqs,rsk->rqk", attn_probs, value_part, preferred_element_type=jnp.float32
-    ).astype(jnp.bfloat16)
-    by_head = head_out.reshape(local_tokens, devices, head_dev * HD).transpose(1, 0, 2)
+    grouped = (local_tokens, kv_heads, slots, 2 * HD)
+    written = lax.broadcasted_iota(jnp.int32, grouped, 2) == (own_pos + SINK)[:, None, None, None]
+    new_cache = jnp.where(
+        written,
+        new_kv.reshape(local_tokens, kv_heads, 1, 2 * HD),
+        kv_cache.reshape(grouped),
+    ).reshape(kv_cache.shape)
     hidden_out = layer(
         devices,
-        by_head,
+        queries,
         hidden_in,
         norm_gain.reshape(1, -1),
         route_logits,
         expert_ids,
+        new_cache,
         (out_weight, expert_in, expert_out),
     )
     return (hidden_out, new_cache)

time: 49 us -> 44.4 us (0.906)
  Pallas kernels: 40.9 us -> 38.8 us
  local copies, waits for them, and re-layouts: 3.28 us -> 1.53 us
  matrix products: 1.34 us -> 0 us
  other arithmetic: 2.55 us -> 3.23 us
    pallas_call x1, Pallas kernels: 40.9 us -> 38.8 us  [layer(): pl.pallas_call(functools.partial(layer_kernel, n), out_shape=jax.ShapeDty...]
    dot_general x2 -> x0, matrix products: 1.34 us -> none  [the longest x1 0.96 us: on_device(): jnp.einsum('rqs,rsk->rqk', attn_probs, value_part, preferred_element_type...]
    select_n x1, other arithmetic: 1.51 us -> 2.5 us  [on_device(): jnp.where(written, new_kv.reshape(local_tokens, kv_heads, 1, 2 * HD), kv_...]
    unnamed x4 -> x1, local copies, waits for them, and re-layouts: 2.31 us -> 1.38 us
    reshape x2 -> x0, local copies, waits for them, and re-layouts: 0.82 us -> none  [on_device(): head_out.reshape(local_tokens, devices, head_dev * HD).transpose(1, 0, 2)]
where the time goes in v2:
time: 44.4 us; the launch traced here: 44.2 us
  Pallas kernels  38.8 us (87%)
  other arithmetic  3.23 us (7%)
  local copies, waits for them, and re-layouts  1.53 us (3%)
  between operations  0.64 us (1%)
    pallas_call x1, Pallas kernels, layer(): pl.pallas_call(functools.partial(layer_kernel, n), out_shape=jax.ShapeDty...  38.8 us
    select_n x1, other arithmetic, on_device(): jnp.where(written, new_kv.reshape(local_tokens, kv_heads, 1, 2 * HD), kv_...  2.5 us
    unnamed x1, local copies, waits for them, and re-layouts  1.38 us

profile of v2, /device:TPU:0, one launch (start us, length us, event | category | flops | bytes accessed | tf_op | source)
XLA Modules:
  0.0 44.2 jit_solution(4765371459273101523)
XLA Ops:
  0.6 0.7 %dynamic-slice_add_fusion = s32[8]{0:T(128)S(1)} fusion(s32[128]{0:T(128)} %param.15, s32[]{:T(128)S(6)} %select_n.8), kind=kLoop, calls=%fused_computation.2 | loop fusion | flops 8 | bytes 68 | tf_op jit(solution)/shard_map/add | solution.py:362
  1.4 0.1 eq.13
  1.4 0.1 eq.14
  1.5 2.5 %fusion.new_cache = bf16[32,64,256]{2,1,0:T(8,128)(2,1)} fusion(bf16[32,64,256]{2,1,0:T(8,128)(2,1)} %param.13, s32[32]{0:T(128)S(1)} %eq.14, bf16[32,256]{1,0:T(8,128)(2,1)} %param.14), kind=kLoop, calls=%fused_computation.1 | loop fusion | flops 1048576 | bytes 2113664 | tf_op jit(solution)/shard_map/jit(_where)/select_n | solution.py:363
  4.0 38.8 %layer.1 = bf16[8,2048]{1,0:T(8,128)(2,1)} custom-call(bf16[32,2048]{1,0:T(8,128)(2,1)} %queries.1, bf16[8,2048]{1,0:T(8,128)(2,1)} %hidden_in.1, f32[1,2048]{1,0:T(1,128)} %bitcast.1, f32[8,8]{1,0:T(8,128)} %route_logits.1, s32[8,8]{1,0:T(8,128)} %expert_ids.1, bf16[32,64,256]{2,1,0:T(8,128)(2,1)} %fusion.new_cache, bf16[512,2048]{1,0:T(8,128)(2,1)} %out_weight.1, ...), custom_call_target="tpu_custom_call" | custom-call | tf_op jit(solution)/shard_map/layer/pallas_call | solution.py:291
  42.8 1.4 %copy.14 = bf16[8,2048]{1,0:T(8,128)(2,1)} copy(bf16[8,2048]{1,0:T(8,128)(2,1)} %layer.1) | data formatting | bytes 65536

commit v3 on v2

--- a/solution.py
+++ b/solution.py
@@ -24,11 +24,14 @@
     norm_gain,
     route_logits,
     expert_ids,
-    new_cache,
+    new_kv,
+    cycle_pos,
+    kv_cache,
     out_weight,
     expert_in,
     expert_out,
     hidden_out,
+    new_cache,
     w_proj,
     w_in,
     w_out,
@@ -73,7 +76,7 @@
             barrier, inc=1, device_id={"tensor": lax.rem(me + k, n)}, device_id_type=MESH
         )
 
-    cache_load = pltpu.make_async_copy(new_cache, cache, load_sem.at[3])
+    cache_load = pltpu.make_async_copy(kv_cache, cache, load_sem.at[3])
     cache_load.start()
     loads = [
         pltpu.make_async_copy(out_weight, w_proj, load_sem.at[0]),
@@ -91,6 +94,13 @@
             :, h * HD : (h + 1) * HD
         ].astype(jnp.float32)
     cache_load.wait()
+    slot_ids = lax.broadcasted_iota(jnp.int32, cache.shape[1:], 0)
+    for t in range(tokens):
+        written = slot_ids == cycle_pos[me * tokens + t] + SINK
+        for r in range(t * kv_heads, (t + 1) * kv_heads):
+            cache[r] = jnp.where(
+                written, new_kv[r : r + 1, :].astype(jnp.float32), cache[r].astype(jnp.float32)
+            ).astype(jnp.bfloat16)
     for r in range(rows_here):
         query = query_rows[pl.ds(r, per_kv, stride=rows_here), :].astype(jnp.bfloat16)
         score_rows[r * per_kv : (r + 1) * per_kv, :] = lax.dot_general(
@@ -102,6 +112,8 @@
     scores = score_rows[...] / math.sqrt(HD)
     powers = jnp.exp(scores - jnp.max(scores, axis=-1, keepdims=True))
     score_rows[...] = powers / jnp.sum(powers, axis=-1, keepdims=True)
+    cache_store = pltpu.make_async_copy(cache, new_cache, load_sem.at[4])
+    cache_store.start()
     for r in range(rows_here):
         probs = score_rows[r * per_kv : (r + 1) * per_kv, :].astype(jnp.bfloat16)
         first = (r % kv_heads) * per_kv * tokens + r // kv_heads
@@ -267,6 +279,7 @@
     moe_total = reduce_scatter(1, lambda: expert_term(0), lambda: expert_term(half))
     hidden_out[...] = (mid_wide + moe_total).astype(jnp.bfloat16)
 
+    cache_store.wait()
     wait_bytes(heads.at[pl.ds(0, n - 1)], head_send)
     for r in range(2):
         core_copy(r).wait_send()
@@ -275,13 +288,13 @@
     wait_bytes(gathered.at[pl.ds(0, chips)], relay_send)
 
 
-def layer(n, queries, hidden_in, norm_gain, route_logits, expert_ids, new_cache, weights):
+def layer(n, queries, hidden_in, norm_gain, route_logits, expert_ids, new_kv, cycle_pos, kv_cache, weights):
     tokens, width = hidden_in.shape
     out_weight, expert_in, expert_out = weights
     ff = expert_out.shape[1]
     chips = n // 2
     pad = -(-n // 128) * 128
-    rows_here, slots, _ = new_cache.shape
+    rows_here, slots, _ = kv_cache.shape
     heads_all = rows_here // tokens * (queries.shape[1] // HD)
     exchange = (n, heads_all // n, tokens, HD)
     bf16, f32 = jnp.bfloat16, jnp.float32
@@ -290,14 +303,17 @@
     dma = pltpu.SemaphoreType.DMA
     return pl.pallas_call(
         functools.partial(layer_kernel, n),
-        out_shape=jax.ShapeDtypeStruct((tokens, width), bf16),
-        in_specs=[vmem] * 5 + [hbm] * 4,
-        out_specs=vmem,
+        out_shape=(
+            jax.ShapeDtypeStruct((tokens, width), bf16),
+            jax.ShapeDtypeStruct(kv_cache.shape, bf16),
+        ),
+        in_specs=[vmem] * 6 + [pl.BlockSpec(memory_space=pltpu.SMEM)] + [hbm] * 4,
+        out_specs=(vmem, hbm),
         scratch_shapes=[
             pltpu.VMEM(out_weight.shape, bf16),
             pltpu.VMEM(expert_in.shape[1:], bf16),
             pltpu.VMEM(expert_out.shape[1:], bf16),
-            pltpu.VMEM(new_cache.shape, bf16),
+            pltpu.VMEM(kv_cache.shape, bf16),
             pltpu.VMEM((heads_all * tokens, HD), f32),
             pltpu.VMEM((heads_all * tokens, slots), f32),
             pltpu.VMEM((heads_all * tokens, HD), f32),
@@ -310,7 +326,7 @@
             pltpu.VMEM((2, chips, tokens, width), bf16),
             pltpu.VMEM((n, tokens, width + pad), bf16),
             pltpu.VMEM((n * tokens, ff), bf16),
-            dma((4,)),
+            dma((5,)),
             dma,
             dma,
             dma((2,)),
@@ -332,7 +348,9 @@
         norm_gain,
         route_logits,
         expert_ids,
-        new_cache,
+        new_kv,
+        cycle_pos,
+        kv_cache,
         out_weight,
         expert_in,
         expert_out,
@@ -353,29 +371,18 @@
     expert_out,
 ):
     devices = lax.axis_size("tensor")
-    device_index = lax.axis_index("tensor")
-    rows_here, slots, _ = kv_cache.shape
-    local_tokens = hidden_in.shape[0]
-    kv_heads = rows_here // local_tokens
-    own_pos = lax.dynamic_slice_in_dim(cycle_pos, device_index * local_tokens, local_tokens)
-    grouped = (local_tokens, kv_heads, slots, 2 * HD)
-    written = lax.broadcasted_iota(jnp.int32, grouped, 2) == (own_pos + SINK)[:, None, None, None]
-    new_cache = jnp.where(
-        written,
-        new_kv.reshape(local_tokens, kv_heads, 1, 2 * HD),
-        kv_cache.reshape(grouped),
-    ).reshape(kv_cache.shape)
-    hidden_out = layer(
+    return layer(
         devices,
         queries,
         hidden_in,
         norm_gain.reshape(1, -1),
         route_logits,
         expert_ids,
-        new_cache,
+        new_kv,
+        cycle_pos,
+        kv_cache,
         (out_weight, expert_in, expert_out),
     )
-    return (hidden_out, new_cache)
 
 
 def solution(mesh):

time: 44.4 us -> 43.6 us (0.982)
  other arithmetic: 3.23 us -> 0 us
  local copies, waits for them, and re-layouts: 1.53 us -> 3.68 us
    select_n x1 -> x0, other arithmetic: 2.5 us -> none  [on_device(): jnp.where(written, new_kv.reshape(local_tokens, kv_heads, 1, 2 * HD), kv_...]
    unnamed x1 -> x2, local copies, waits for them, and re-layouts: 1.38 us -> 3.68 us
    add x1 -> x0, other arithmetic: 0.73 us -> none  [on_device(): own_pos + SINK]
where the time goes in v3:
time: 43.6 us; the launch traced here: 43.4 us
  Pallas kernels  39 us (89%)
  local copies, waits for them, and re-layouts  3.68 us (8%)
  between operations  0.64 us (1%)
    pallas_call x1, Pallas kernels, layer(): pl.pallas_call(functools.partial(layer_kernel, n), out_shape=(jax.ShapeDt...  39 us
    unnamed x2, local copies, waits for them, and re-layouts  3.68 us

profile of v3, /device:TPU:0, one launch (start us, length us, event | category | flops | bytes accessed | tf_op | source)
XLA Modules:
  0.0 43.4 jit_solution(4822060793855482564)
XLA Ops:
  0.6 39.0 %layer.1 = (bf16[8,2048]{1,0:T(8,128)(2,1)}, bf16[32,64,256]{2,1,0:T(8,128)(2,1)}) custom-call(bf16[32,2048]{1,0:T(8,128)(2,1)} %queries.1, bf16[8,2048]{1,0:T(8,128)(2,1)} %hidden_in.1, f32[1,2048]{1,0:T(1,128)} %bitcast.1, f32[8,8]{1,0:T(8,128)} %route_logits.1, s32[8,8]{1,0:T(8,128)} %expert_ids.1, bf16[32,256]{1,0:T(8,128)(2,1)} %new_kv.1, ...), custom_call_target="tpu_custom_call" | custom-call | tf_op jit(solution)/shard_map/layer/pallas_call | solution.py:304
  39.7 1.4 %copy.15 = bf16[8,2048]{1,0:T(8,128)(2,1)} copy(bf16[8,2048]{1,0:T(8,128)(2,1)} %get-tuple-element.4) | data formatting | bytes 65536
  41.1 2.3 %copy.16 = bf16[32,64,256]{2,1,0:T(8,128)(2,1)} copy(bf16[32,64,256]{2,1,0:T(8,128)(2,1)} %get-tuple-element.5) | data formatting | bytes 2097152
